TPU v7x, 32 devices: a whole 2x2x4 slice. The times are simulated.
32 devices in a mesh: visit: 2 (over x), patch: 16 (over z, y, core).
Axes of the slice: x: 2, y: 2, z: 4, core: 2. Of those that a mesh axis runs over, the one named last changes fastest.
Arguments:
- images: bfloat16 [2, 96, 128, 512], P('visit', 'patch'), may hold values from -12 to 12
- coefficients: float32 [2, 96, 3, 40], P('visit', 'patch'), may hold values from -2 to 2
- intersection: int32 [2, 96, 2], P('visit'), may hold values from 0 to 15, as said below
- row_offset: int32 [2, 96], P('visit'), may hold values from 0 to 7
- col_offset: int32 [2, 96], P('visit'), may hold values from 0 to 511
- shifts: float32 [2, 96, 2], P('visit'), may hold values from 0 to 1
- inv_var: float32 [2, 96], P('visit'), may hold values from 0.3 to 3
Outputs:
- coadd: float32 [128, 8192], P('visit', 'patch')
- detection: float32 [128, 8192], P('visit', 'patch')
Inputs may be any that keep to these rules, and one draw needn't show every extreme that they name: intersection[v, c, 1] = intersection[v, c, 0] + 1. Within each aligned block of 6 exposures of a visit (c from b * 6 to (b + 1) * 6 - 1), no patch is named twice.
All inputs are finite; a program needn't handle non-finite values.
Results may differ from a plain program's by a relative error of at most 0.0061.
Values may be sent and summed in bfloat16 or wider, within the bound.
No kernel may reach another device: no remote copies, remote signals or barrier semaphores. Data moves between devices by JAX's collectives and lax.ppermute only.
A program may use at most 128 MiB of HBM per device.

v0:
```python
import jax
import jax.numpy as jnp
from jax import lax
from jax.sharding import PartitionSpec as P

KRAD = 10
DRAD = 4
WIDTHS_PX = (1.0, 1.7, 2.6, 3.6)


def extended(array, sides, width):
    for axis, dim in sides:
        peers, length = (lax.axis_size(axis), array.shape[dim])
        up = [(i, (i + 1) % peers) for i in range(peers - 1)]
        down = [(j, i) for i, j in up]
        last = lax.slice_in_dim(array, length - width, length, axis=dim)
        initial = lax.slice_in_dim(array, 0, width, axis=dim)
        before = lax.ppermute(last, axis, up)
        after = lax.ppermute(initial, axis, down)
        array = jnp.concatenate([before, array, after], axis=dim)
    return array


def kernel_value(offsets, width_px, degree):
    scaled = offsets / width_px
    return scaled**degree * jnp.exp(-offsets * offsets / (2.0 * width_px * width_px))


def band_tables(radius, extent):
    offsets = jnp.arange(-radius, radius + 1).astype(jnp.float32)
    distance = (jnp.arange(extent)[None, :] - jnp.arange(extent)[:, None]).astype(jnp.float32)
    inside = jnp.abs(distance) <= radius
    tables = []
    for group in range(4):
        for degree in range(4):
            profile = kernel_value(offsets, WIDTHS_PX[group], degree)
            norm_value = jnp.sqrt(jnp.sum(profile * profile))
            values = kernel_value(distance, WIDTHS_PX[group], degree) / norm_value
            tables.append(jnp.where(inside, values, 0.0).astype(jnp.bfloat16))
    return jnp.stack(tables).reshape(4, 4, extent, extent)


def match_exposure(exposure, weights, row_band, col_band, row_pos, col_pos):
    smoothed = jnp.einsum(
        "gdri,iw->gdrw", row_band, exposure, preferred_element_type=jnp.float32
    ).astype(jnp.bfloat16)
    matched = jnp.zeros(exposure.shape, jnp.float32)
    term = 0
    for group in range(4):
        for x_degree in range(4):
            count = 4 - x_degree
            response = jnp.einsum(
                "drw,xw->drx",
                smoothed[group, :count],
                col_band[group, x_degree],
                preferred_element_type=jnp.float32,
            )
            picked = weights[:, term : term + count]
            steady = jnp.sum(picked[0][:, None, None] * response, 0)
            along_rows = jnp.sum(picked[1][:, None, None] * response, 0)
            along_cols = jnp.sum(picked[2][:, None, None] * response, 0)
            matched = (
                matched + steady + row_pos[:, None] * along_rows + col_pos[None, :] * along_cols
            )
            term += count
    return matched.astype(jnp.bfloat16)


def warp_exposure(exposure, row_shift, col_shift, frac_row, frac_col, weight):
    row_count, col_count = exposure.shape
    nothing = jnp.zeros((), jnp.bfloat16)
    upper = (1.0 - frac_row).astype(jnp.bfloat16)
    lower = frac_row.astype(jnp.bfloat16)
    left = (1.0 - frac_col).astype(jnp.bfloat16)
    right = frac_col.astype(jnp.bfloat16)
    target_row = jnp.arange(row_count)[:, None]
    source_row = jnp.arange(row_count)[None, :]
    row_map = jnp.where(source_row == target_row - row_shift, upper, nothing) + jnp.where(
        source_row == target_row - row_shift - 1, lower, nothing
    )
    source_col = jnp.arange(col_count)[:, None]
    target_col = jnp.arange(col_count)[None, :]
    col_map = jnp.where(source_col == target_col - col_shift, left, nothing) + jnp.where(
        source_col == target_col - col_shift - 1, right, nothing
    )
    middle = jnp.dot(row_map, exposure, preferred_element_type=jnp.float32).astype(jnp.bfloat16)
    warped = jnp.dot(middle, col_map, preferred_element_type=jnp.float32)
    row_cover = jnp.sum(row_map.astype(jnp.float32), 1)
    col_cover = jnp.sum(col_map.astype(jnp.float32), 0)
    return (weight * warped, weight * row_cover[:, None] * col_cover[None, :])


def detect(framed, radius):
    offsets = jnp.arange(-radius, radius + 1).astype(jnp.float32)
    profile = jnp.exp(-offsets * offsets / 8.0)
    profile = profile / jnp.sqrt(jnp.sum(profile * profile))
    row_count = framed.shape[0] - 2 * radius
    col_count = framed.shape[1] - 2 * radius
    across = jnp.zeros((row_count, framed.shape[1]), jnp.float32)
    for tap_idx in range(2 * radius + 1):
        across = across + profile[tap_idx] * framed[tap_idx : tap_idx + row_count]
    result = jnp.zeros((row_count, col_count), jnp.float32)
    for tap_idx in range(2 * radius + 1):
        result = result + profile[tap_idx] * across[:, tap_idx : tap_idx + col_count]
    return result


def local(images, coefficients, intersection, row_offset, col_offset, shifts, inv_var):
    exposures = images[0]
    weights_all = coefficients[0]
    row_count = exposures.shape[1]
    col_count = exposures.shape[2]
    table = intersection[0]
    row_shifts = row_offset[0]
    col_shifts = col_offset[0]
    fractions = shifts[0]
    inverse = inv_var[0]
    own_patch = lax.axis_index("patch")
    row_band = band_tables(KRAD, row_count)
    col_band = band_tables(KRAD, col_count)
    row_pos = (2.0 * jnp.arange(row_count).astype(jnp.float32) + 1.0) / row_count - 1.0
    col_pos = (2.0 * jnp.arange(col_count).astype(jnp.float32) + 1.0) / col_count - 1.0
    matched = lax.map(
        lambda operands: match_exposure(
            operands[0], operands[1], row_band, col_band, row_pos, col_pos
        ),
        (exposures, weights_all),
    )
    empty = (
        jnp.zeros((row_count, col_count), jnp.float32),
        jnp.zeros((row_count, col_count), jnp.float32),
    )

    def add_exposure(totals, exposure, ccd, hit_first):
        col_shift = jnp.where(hit_first, col_shifts[ccd], col_shifts[ccd] - col_count)
        flux_part, cover_part = warp_exposure(
            exposure, row_shifts[ccd], col_shift, fractions[ccd, 0], fractions[ccd, 1], inverse[ccd]
        )
        return (totals[0] + flux_part, totals[1] + cover_part)

    arrived = lax.all_gather(matched, "patch", axis=0, tiled=True)

    def visit_one(offset, inner):
        hit_first = table[offset, 0] == own_patch
        hit_second = table[offset, 1] == own_patch
        exposure = lax.dynamic_index_in_dim(arrived, offset, 0, keepdims=False)
        return lax.cond(
            hit_first | hit_second,
            lambda: add_exposure(inner, exposure, offset, hit_first),
            lambda: inner,
        )

    flux_sum, cover_sum = lax.fori_loop(0, arrived.shape[0], visit_one, empty)
    flux_part, cover_part = (
        lax.psum_scatter(flux_sum, "visit", scatter_dimension=0, tiled=True),
        lax.psum_scatter(cover_sum, "visit", scatter_dimension=0, tiled=True),
    )
    coadd = flux_part / jnp.maximum(cover_part, 1.0)
    framed = extended(coadd, (("visit", 0), ("patch", 1)), DRAD)
    detection = detect(framed, DRAD)
    return (coadd, detection)


def solution(mesh):
    return jax.shard_map(
        local,
        mesh=mesh,
        in_specs=(
            P("visit", "patch", None, None),
            P("visit", "patch", None, None),
            P("visit", None, None),
            P("visit", None),
            P("visit", None),
            P("visit", None, None),
            P("visit", None),
        ),
        out_specs=(P("visit", "patch"), P("visit", "patch")),
        check_vma=False,
    )
```

profile of v0, /device:TPU:5, one launch (start us, length us, event | category | flops | bytes accessed | tf_op | source)
XLA Modules:
  0.0 671.8 jit_solution(11030103022260496552)
XLA Ops:
  51.3 119.2 %while.28 = (s32[]{:T(128)}, bf16[6,128,512]{2,1,0:T(8,128)(2,1)S(1)}, f32[6,3,40]{2,1,0:T(4,128)S(1)}, bf16[6,128,512]{1,2,0:T(8,128)(2,1)S(1)}, bf16[4,4,128,1...) while((s32[]{:T(128)}, ...), condition=%wide.region_53.54_spmd.clone.clone, body=%wide.region_16.53_spmd.clone.clone.sunk | while | flops 2971667456 | bytes 70542368 | solution.py:123
  62.8 8.5 %fusion.219 = bf16[6,128,512]{2,1,0:T(8,128)(2,1)S(1)} fusion(bf16[6,128,512]{2,1,0:T(8,128)(2,1)S(1)} %get-tuple-element.857, s32[]{:T(128)} %get-tuple-element.856, bf16[4,4,512,512]{3,2,1,0:T(8,128)(2,1)S(1)} %copy-done, f32[128,512]{1,0:T(8,128)S(1)} %get-tuple-element.764, f32[128,512]{1,0:T(8,128)S(1)} %get-tuple-element.765, ...), kind=kOutput, calls=%fused_computation.133.clone.1 | convolution fusion | flops 73138176 | bytes 11012660 | tf_op jit(solution)/shard_map/while/body/eval_jaxpr/drw,xw->drx/dot_general | solution.py:52
  82.6 8.5 %fusion.219 = bf16[6,128,512]{2,1,0:T(8,128)(2,1)S(1)} fusion(bf16[6,128,512]{2,1,0:T(8,128)(2,1)S(1)} %get-tuple-element.857, s32[]{:T(128)} %get-tuple-element.856, bf16[4,4,512,512]{3,2,1,0:T(8,128)(2,1)S(1)} %copy-done, f32[128,512]{1,0:T(8,128)S(1)} %get-tuple-element.764, f32[128,512]{1,0:T(8,128)S(1)} %get-tuple-element.765, ...), kind=kOutput, calls=%fused_computation.133.clone.1 | convolution fusion | flops 73138176 | bytes 11012660 | tf_op jit(solution)/shard_map/while/body/eval_jaxpr/drw,xw->drx/dot_general | solution.py:52
  102.4 8.5 %fusion.219 = bf16[6,128,512]{2,1,0:T(8,128)(2,1)S(1)} fusion(bf16[6,128,512]{2,1,0:T(8,128)(2,1)S(1)} %get-tuple-element.857, s32[]{:T(128)} %get-tuple-element.856, bf16[4,4,512,512]{3,2,1,0:T(8,128)(2,1)S(1)} %copy-done, f32[128,512]{1,0:T(8,128)S(1)} %get-tuple-element.764, f32[128,512]{1,0:T(8,128)S(1)} %get-tuple-element.765, ...), kind=kOutput, calls=%fused_computation.133.clone.1 | convolution fusion | flops 73138176 | bytes 11012660 | tf_op jit(solution)/shard_map/while/body/eval_jaxpr/drw,xw->drx/dot_general | solution.py:52
  122.3 8.5 %fusion.219 = bf16[6,128,512]{2,1,0:T(8,128)(2,1)S(1)} fusion(bf16[6,128,512]{2,1,0:T(8,128)(2,1)S(1)} %get-tuple-element.857, s32[]{:T(128)} %get-tuple-element.856, bf16[4,4,512,512]{3,2,1,0:T(8,128)(2,1)S(1)} %copy-done, f32[128,512]{1,0:T(8,128)S(1)} %get-tuple-element.764, f32[128,512]{1,0:T(8,128)S(1)} %get-tuple-element.765, ...), kind=kOutput, calls=%fused_computation.133.clone.1 | convolution fusion | flops 73138176 | bytes 11012660 | tf_op jit(solution)/shard_map/while/body/eval_jaxpr/drw,xw->drx/dot_general | solution.py:52
  142.1 8.5 %fusion.219 = bf16[6,128,512]{2,1,0:T(8,128)(2,1)S(1)} fusion(bf16[6,128,512]{2,1,0:T(8,128)(2,1)S(1)} %get-tuple-element.857, s32[]{:T(128)} %get-tuple-element.856, bf16[4,4,512,512]{3,2,1,0:T(8,128)(2,1)S(1)} %copy-done, f32[128,512]{1,0:T(8,128)S(1)} %get-tuple-element.764, f32[128,512]{1,0:T(8,128)S(1)} %get-tuple-element.765, ...), kind=kOutput, calls=%fused_computation.133.clone.1 | convolution fusion | flops 73138176 | bytes 11012660 | tf_op jit(solution)/shard_map/while/body/eval_jaxpr/drw,xw->drx/dot_general | solution.py:52
  161.9 8.5 %fusion.219 = bf16[6,128,512]{2,1,0:T(8,128)(2,1)S(1)} fusion(bf16[6,128,512]{2,1,0:T(8,128)(2,1)S(1)} %get-tuple-element.857, s32[]{:T(128)} %get-tuple-element.856, bf16[4,4,512,512]{3,2,1,0:T(8,128)(2,1)S(1)} %copy-done, f32[128,512]{1,0:T(8,128)S(1)} %get-tuple-element.764, f32[128,512]{1,0:T(8,128)S(1)} %get-tuple-element.765, ...), kind=kOutput, calls=%fused_computation.133.clone.1 | convolution fusion | flops 73138176 | bytes 11012660 | tf_op jit(solution)/shard_map/while/body/eval_jaxpr/drw,xw->drx/dot_general | solution.py:52
  171.5 101.2 %all-gather.2.cloned.1.call-done = bf16[96,128,512]{2,1,0:T(8,128)(2,1)} async-done(((bf16[6,128,512]{2,1,0:T(8,128)(2,1)}), bf16[96,128,512]{2,1,0:T(8,128)(2,1)}) %all-gather.2.cloned.1.call-update) | async-done | bytes 12582928 | tf_op jit(solution)/shard_map/all_gather | solution.py:141
  272.8 335.8 %while.27 = (s32[]{:T(128)}, f32[128,512]{1,0:T(8,128)S(1)}, f32[128,512]{1,0:T(8,128)S(1)}, s32[96,2]{0,1:T(2,128)S(1)}, s32[]{:T(128)}, /*index=5*/f32[96]{0:T...) while((s32[]{:T(128)}, f32[128,512]{1,0:T(8,128)S(1)}, ...), condition=%wide.region_59.60_spmd, body=%wide.region_54.59_spmd.sunk | while | flops 88949520 | bytes 1204658 | solution.py:153
  282.8 9.6 %conditional.2 = ((f32[128,512]{1,0:T(8,128)S(1)}, f32[128,512]{1,0:T(8,128)S(1)})) conditional(s32[]{:T(128)} %convert_element_type.1283, (f32[128,512]{1,0:T(8,128)S(1)}, f32[128,512]{1,0:T(8,128)S(1)}) %tuple.161, (s32[]{:T(128)}, f32[96]{0:T(128)S(1)}, s32[96]{0:T(128)S(1)}, f32[96,2]{0,1:T(2,128)S(1)}, bf16[96,128,512]{2,1,0:T(8,128)(2,1)}, ...), branch_computations={%region_55.55_spmd, %region_56.58_spmd} | conditional | flops 88949512 | bytes 1204415 | solution.py:147
  318.3 9.6 %conditional.2 = ((f32[128,512]{1,0:T(8,128)S(1)}, f32[128,512]{1,0:T(8,128)S(1)})) conditional(s32[]{:T(128)} %convert_element_type.1283, (f32[128,512]{1,0:T(8,128)S(1)}, f32[128,512]{1,0:T(8,128)S(1)}) %tuple.161, (s32[]{:T(128)}, f32[96]{0:T(128)S(1)}, s32[96]{0:T(128)S(1)}, f32[96,2]{0,1:T(2,128)S(1)}, bf16[96,128,512]{2,1,0:T(8,128)(2,1)}, ...), branch_computations={%region_55.55_spmd, %region_56.58_spmd} | conditional | flops 88949512 | bytes 1204415 | solution.py:147
  337.9 9.6 %conditional.2 = ((f32[128,512]{1,0:T(8,128)S(1)}, f32[128,512]{1,0:T(8,128)S(1)})) conditional(s32[]{:T(128)} %convert_element_type.1283, (f32[128,512]{1,0:T(8,128)S(1)}, f32[128,512]{1,0:T(8,128)S(1)}) %tuple.161, (s32[]{:T(128)}, f32[96]{0:T(128)S(1)}, s32[96]{0:T(128)S(1)}, f32[96,2]{0,1:T(2,128)S(1)}, bf16[96,128,512]{2,1,0:T(8,128)(2,1)}, ...), branch_computations={%region_55.55_spmd, %region_56.58_spmd} | conditional | flops 88949512 | bytes 1204415 | solution.py:147
  357.5 9.6 %conditional.2 = ((f32[128,512]{1,0:T(8,128)S(1)}, f32[128,512]{1,0:T(8,128)S(1)})) conditional(s32[]{:T(128)} %convert_element_type.1283, (f32[128,512]{1,0:T(8,128)S(1)}, f32[128,512]{1,0:T(8,128)S(1)}) %tuple.161, (s32[]{:T(128)}, f32[96]{0:T(128)S(1)}, s32[96]{0:T(128)S(1)}, f32[96,2]{0,1:T(2,128)S(1)}, bf16[96,128,512]{2,1,0:T(8,128)(2,1)}, ...), branch_computations={%region_55.55_spmd, %region_56.58_spmd} | conditional | flops 88949512 | bytes 1204415 | solution.py:147
  377.1 9.6 %conditional.2 = ((f32[128,512]{1,0:T(8,128)S(1)}, f32[128,512]{1,0:T(8,128)S(1)})) conditional(s32[]{:T(128)} %convert_element_type.1283, (f32[128,512]{1,0:T(8,128)S(1)}, f32[128,512]{1,0:T(8,128)S(1)}) %tuple.161, (s32[]{:T(128)}, f32[96]{0:T(128)S(1)}, s32[96]{0:T(128)S(1)}, f32[96,2]{0,1:T(2,128)S(1)}, bf16[96,128,512]{2,1,0:T(8,128)(2,1)}, ...), branch_computations={%region_55.55_spmd, %region_56.58_spmd} | conditional | flops 88949512 | bytes 1204415 | solution.py:147
  394.7 9.6 %conditional.2 = ((f32[128,512]{1,0:T(8,128)S(1)}, f32[128,512]{1,0:T(8,128)S(1)})) conditional(s32[]{:T(128)} %convert_element_type.1283, (f32[128,512]{1,0:T(8,128)S(1)}, f32[128,512]{1,0:T(8,128)S(1)}) %tuple.161, (s32[]{:T(128)}, f32[96]{0:T(128)S(1)}, s32[96]{0:T(128)S(1)}, f32[96,2]{0,1:T(2,128)S(1)}, bf16[96,128,512]{2,1,0:T(8,128)(2,1)}, ...), branch_computations={%region_55.55_spmd, %region_56.58_spmd} | conditional | flops 88949512 | bytes 1204415 | solution.py:147
  416.3 9.6 %conditional.2 = ((f32[128,512]{1,0:T(8,128)S(1)}, f32[128,512]{1,0:T(8,128)S(1)})) conditional(s32[]{:T(128)} %convert_element_type.1283, (f32[128,512]{1,0:T(8,128)S(1)}, f32[128,512]{1,0:T(8,128)S(1)}) %tuple.161, (s32[]{:T(128)}, f32[96]{0:T(128)S(1)}, s32[96]{0:T(128)S(1)}, f32[96,2]{0,1:T(2,128)S(1)}, bf16[96,128,512]{2,1,0:T(8,128)(2,1)}, ...), branch_computations={%region_55.55_spmd, %region_56.58_spmd} | conditional | flops 88949512 | bytes 1204415 | solution.py:147
  437.9 9.6 %conditional.2 = ((f32[128,512]{1,0:T(8,128)S(1)}, f32[128,512]{1,0:T(8,128)S(1)})) conditional(s32[]{:T(128)} %convert_element_type.1283, (f32[128,512]{1,0:T(8,128)S(1)}, f32[128,512]{1,0:T(8,128)S(1)}) %tuple.161, (s32[]{:T(128)}, f32[96]{0:T(128)S(1)}, s32[96]{0:T(128)S(1)}, f32[96,2]{0,1:T(2,128)S(1)}, bf16[96,128,512]{2,1,0:T(8,128)(2,1)}, ...), branch_computations={%region_55.55_spmd, %region_56.58_spmd} | conditional | flops 88949512 | bytes 1204415 | solution.py:147
  465.4 9.6 %conditional.2 = ((f32[128,512]{1,0:T(8,128)S(1)}, f32[128,512]{1,0:T(8,128)S(1)})) conditional(s32[]{:T(128)} %convert_element_type.1283, (f32[128,512]{1,0:T(8,128)S(1)}, f32[128,512]{1,0:T(8,128)S(1)}) %tuple.161, (s32[]{:T(128)}, f32[96]{0:T(128)S(1)}, s32[96]{0:T(128)S(1)}, f32[96,2]{0,1:T(2,128)S(1)}, bf16[96,128,512]{2,1,0:T(8,128)(2,1)}, ...), branch_computations={%region_55.55_spmd, %region_56.58_spmd} | conditional | flops 88949512 | bytes 1204415 | solution.py:147
  487.0 9.6 %conditional.2 = ((f32[128,512]{1,0:T(8,128)S(1)}, f32[128,512]{1,0:T(8,128)S(1)})) conditional(s32[]{:T(128)} %convert_element_type.1283, (f32[128,512]{1,0:T(8,128)S(1)}, f32[128,512]{1,0:T(8,128)S(1)}) %tuple.161, (s32[]{:T(128)}, f32[96]{0:T(128)S(1)}, s32[96]{0:T(128)S(1)}, f32[96,2]{0,1:T(2,128)S(1)}, bf16[96,128,512]{2,1,0:T(8,128)(2,1)}, ...), branch_computations={%region_55.55_spmd, %region_56.58_spmd} | conditional | flops 88949512 | bytes 1204415 | solution.py:147
  512.6 9.6 %conditional.2 = ((f32[128,512]{1,0:T(8,128)S(1)}, f32[128,512]{1,0:T(8,128)S(1)})) conditional(s32[]{:T(128)} %convert_element_type.1283, (f32[128,512]{1,0:T(8,128)S(1)}, f32[128,512]{1,0:T(8,128)S(1)}) %tuple.161, (s32[]{:T(128)}, f32[96]{0:T(128)S(1)}, s32[96]{0:T(128)S(1)}, f32[96,2]{0,1:T(2,128)S(1)}, bf16[96,128,512]{2,1,0:T(8,128)(2,1)}, ...), branch_computations={%region_55.55_spmd, %region_56.58_spmd} | conditional | flops 88949512 | bytes 1204415 | solution.py:147
  528.2 9.6 %conditional.2 = ((f32[128,512]{1,0:T(8,128)S(1)}, f32[128,512]{1,0:T(8,128)S(1)})) conditional(s32[]{:T(128)} %convert_element_type.1283, (f32[128,512]{1,0:T(8,128)S(1)}, f32[128,512]{1,0:T(8,128)S(1)}) %tuple.161, (s32[]{:T(128)}, f32[96]{0:T(128)S(1)}, s32[96]{0:T(128)S(1)}, f32[96,2]{0,1:T(2,128)S(1)}, bf16[96,128,512]{2,1,0:T(8,128)(2,1)}, ...), branch_computations={%region_55.55_spmd, %region_56.58_spmd} | conditional | flops 88949512 | bytes 1204415 | solution.py:147
  553.8 9.6 %conditional.2 = ((f32[128,512]{1,0:T(8,128)S(1)}, f32[128,512]{1,0:T(8,128)S(1)})) conditional(s32[]{:T(128)} %convert_element_type.1283, (f32[128,512]{1,0:T(8,128)S(1)}, f32[128,512]{1,0:T(8,128)S(1)}) %tuple.161, (s32[]{:T(128)}, f32[96]{0:T(128)S(1)}, s32[96]{0:T(128)S(1)}, f32[96,2]{0,1:T(2,128)S(1)}, bf16[96,128,512]{2,1,0:T(8,128)(2,1)}, ...), branch_computations={%region_55.55_spmd, %region_56.58_spmd} | conditional | flops 88949512 | bytes 1204415 | solution.py:147
  569.4 9.6 %conditional.2 = ((f32[128,512]{1,0:T(8,128)S(1)}, f32[128,512]{1,0:T(8,128)S(1)})) conditional(s32[]{:T(128)} %convert_element_type.1283, (f32[128,512]{1,0:T(8,128)S(1)}, f32[128,512]{1,0:T(8,128)S(1)}) %tuple.161, (s32[]{:T(128)}, f32[96]{0:T(128)S(1)}, s32[96]{0:T(128)S(1)}, f32[96,2]{0,1:T(2,128)S(1)}, bf16[96,128,512]{2,1,0:T(8,128)(2,1)}, ...), branch_computations={%region_55.55_spmd, %region_56.58_spmd} | conditional | flops 88949512 | bytes 1204415 | solution.py:147
  595.0 9.6 %conditional.2 = ((f32[128,512]{1,0:T(8,128)S(1)}, f32[128,512]{1,0:T(8,128)S(1)})) conditional(s32[]{:T(128)} %convert_element_type.1283, (f32[128,512]{1,0:T(8,128)S(1)}, f32[128,512]{1,0:T(8,128)S(1)}) %tuple.161, (s32[]{:T(128)}, f32[96]{0:T(128)S(1)}, s32[96]{0:T(128)S(1)}, f32[96,2]{0,1:T(2,128)S(1)}, bf16[96,128,512]{2,1,0:T(8,128)(2,1)}, ...), branch_computations={%region_55.55_spmd, %region_56.58_spmd} | conditional | flops 88949512 | bytes 1204415 | solution.py:147
  611.4 8.4 %reduce-scatter.3.cloned.1.call-done = f32[64,512]{1,0:T(8,128)} async-done(((f32[128,512]{1,0:T(8,128)}), f32[64,512]{1,0:T(8,128)}) %reduce-scatter.3.cloned.1.call-update) | async-done | bytes 131088 | tf_op jit(solution)/shard_map/reduce_scatter | solution.py:155
  619.7 14.0 %reduce-scatter.5.cloned.1.call-done = f32[64,512]{1,0:T(8,128)} async-done(((f32[128,512]{1,0:T(8,128)}), f32[64,512]{1,0:T(8,128)}) %reduce-scatter.5.cloned.1.call-update) | async-done | bytes 131088 | tf_op jit(solution)/shard_map/reduce_scatter | solution.py:156
  634.8 2.2 collective-permute-start
  638.3 3.1 collective-permute-done.1
  641.4 5.3 collective-permute-start.2
  649.3 3.6 collective-permute-done.3
  653.0 5.7 fusion.128
  658.7 6.5 fusion.136
  (584 shorter events, 261.1 us)
Async XLA Ops:
  7.2 43.7 %copy-start.4 = (bf16[1,6,128,512]{3,2,1,0:T(8,128)(2,1)S(1)}, bf16[1,6,128,512]{3,2,1,0:T(8,128)(2,1)}, u32[]{:S(2)}) copy-start(bf16[1,6,128,512]{3,2,1,0:T(8,128)(2,1)} %param.13) | copy-start | bytes 2359300
  7.2 44.1 %copy-start.8 = (f32[1,6,3,40]{3,0,2,1:T(1,128)S(1)}, f32[1,6,3,40]{3,0,2,1:T(1,128)}, u32[]{:S(2)}) copy-start(f32[1,6,3,40]{3,0,2,1:T(1,128)} %param.14) | copy-start | bytes 8644
  7.2 265.5 %all-gather.2.cloned.1.call-start = ((), (), s32[]{:S(2)}) async-start(), calls=%async_computation.2 | async-start | bytes 13369344 | tf_op jit(solution)/shard_map/all_gather | solution.py:141
  51.3 221.5 %copy-start.6 = (s32[1,96,2]{1,2,0:T(2,128)S(1)}, s32[1,96,2]{1,2,0:T(2,128)}, u32[]{:S(2)}) copy-start(s32[1,96,2]{1,2,0:T(2,128)} %param.15) | copy-start | bytes 2308
  51.3 221.5 %copy-start.7 = (f32[1,96,2]{1,2,0:T(2,128)S(1)}, f32[1,96,2]{1,2,0:T(2,128)}, u32[]{:S(2)}) copy-start(f32[1,96,2]{1,2,0:T(2,128)} %param.18) | copy-start | bytes 2308
  51.3 221.5 %copy-start.9 = (f32[1,96]{1,0:T(1,128)S(1)}, f32[1,96]{1,0:T(1,128)}, u32[]{:S(2)}) copy-start(f32[1,96]{1,0:T(1,128)} %param.19) | copy-start | bytes 1156
  51.3 221.5 %copy-start.10 = (s32[1,96]{1,0:T(1,128)S(1)}, s32[1,96]{1,0:T(1,128)}, u32[]{:S(2)}) copy-start(s32[1,96]{1,0:T(1,128)} %param.16) | copy-start | bytes 1156
  51.3 221.5 %copy-start.11 = (s32[1,96]{1,0:T(1,128)S(1)}, s32[1,96]{1,0:T(1,128)}, u32[]{:S(2)}) copy-start(s32[1,96]{1,0:T(1,128)} %param.17) | copy-start | bytes 1156
  51.5 4.7 copy-start
  71.3 4.7 copy-start
  91.2 4.7 copy-start
  111.0 4.7 copy-start
  130.8 4.7 copy-start
  150.7 4.7 copy-start
  170.5 0.9 copy-start.5
  171.4 448.3 %reduce-scatter.3.cloned.1.call-start = ((), (), s32[]{:S(2)}) async-start(), calls=%async_computation.3 | async-start | bytes 393216 | tf_op jit(solution)/shard_map/reduce_scatter | solution.py:155
  608.6 0.7 copy-start.3
  608.6 0.8 copy-start.1
  609.3 24.4 %reduce-scatter.5.cloned.1.call-start = ((), (), s32[]{:S(2)}) async-start(), calls=%async_computation.4 | async-start | bytes 393216 | tf_op jit(solution)/shard_map/reduce_scatter | solution.py:156
  634.7 30.5 %copy-start.2 = (f32[64,512]{1,0:T(8,128)}, f32[64,512]{1,0:T(8,128)S(1)}, u32[]{:S(2)}) copy-start(f32[64,512]{1,0:T(8,128)S(1)} %maximum_divide_fusion) | copy-start | bytes 393220
  634.8 3.5 collective-permute-start
  636.9 4.4 collective-permute-start.1
  641.4 7.9 %collective-permute-start.2 = (f32[72,4]{1,0:T(8,128)S(1)}, f32[72,4]{1,0:T(8,128)S(1)}, u32[]{:S(2)}, u32[]{:S(2)}) collective-permute-start(f32[72,4]{1,0:T(8,128)S(1)} %get-tuple-element.558), channel_id=1, source_target_pairs={{0,1},{1,2},{2,3},{3,4},{4,5},{5,6},{6,7},{7,8},{8,9},{9,10},{10,1... | collective-permute-start | bytes 3464 | tf_op jit(solution)/shard_map/ppermute | solution.py:18
  646.7 6.2 collective-permute-start.3
Sparse Core Ops, SparseCore 0:
  171.6 101.1 all-gather.1
  609.4 10.2 reduce-scatter.2
  622.0 11.7 reduce-scatter.4
where the time goes:
time: 676 us; the launch traced here: 672 us
  loops' own time  185 us (27%)
  matrix products  141 us (21%)
  waiting for transfers between devices  131 us (19%)
  local copies, waits for them, and re-layouts  107 us (16%)
  other arithmetic  71.6 us (11%)
  between operations  25.4 us (4%)
  starting transfers between devices  10.8 us (2%)
    another operation x1, loops' own time, local(): flux_sum, cover_sum = lax.fori_loop(0, arrived.shape[0], visit_one, empty)  128 us
    dot_general x96, matrix products, match_exposure(): jnp.einsum('drw,xw->drx', smoothed[group, :count], col_band[group, x_degr...  108 us
    all_gather x1, waiting for transfers between devices, local(): arrived = lax.all_gather(matched, 'patch', axis=0, tiled=True)  101 us
    dynamic_slice x96, local copies, waits for them, and re-layouts, visit_one(): hit_second = table[offset, 1] == own_patch  62.7 us
    another operation x96, loops' own time, visit_one(): lax.cond(hit_first | hit_second, lambda: add_exposure(inner, exposure, of...  56 us
    dot_general x15, matrix products, warp_exposure(): warped = jnp.dot(middle, col_map, preferred_element_type=jnp.float32)  28.8 us
    unnamed x30, other arithmetic  21.1 us
    reduce_scatter x1, waiting for transfers between devices, local(): lax.psum_scatter(cover_sum, 'visit', scatter_dimension=0, tiled=True)  14 us
  transfers between devices with their start and end apart: 7, of which 5 were waited for; matrix products, arithmetic and copies ran while one was open for 0% of the time, Pallas kernels for 0%

commit v1 on v0

--- a/solution.py
+++ b/solution.py
@@ -6,6 +6,19 @@
 KRAD = 10
 DRAD = 4
 WIDTHS_PX = (1.0, 1.7, 2.6, 3.6)
+
+
+def ring_gather(shard, axis, dim):
+    ways = lax.axis_size(axis)
+    up = [(d, (d + 1) % ways) for d in range(ways)]
+    down = [(d, (d - 1) % ways) for d in range(ways)]
+    earlier, later = ([shard], [shard])
+    for _ in range(ways // 2):
+        earlier.append(lax.ppermute(earlier[-1], axis, up))
+    for _ in range((ways - 1) // 2):
+        later.append(lax.ppermute(later[-1], axis, down))
+    line = jnp.concatenate([*earlier[::-1], *later[1:]], axis=dim)
+    return jnp.roll(line, (lax.axis_index(axis) - ways // 2) * shard.shape[dim], axis=dim)
 
 
 def extended(array, sides, width):
@@ -138,7 +151,7 @@
         )
         return (totals[0] + flux_part, totals[1] + cover_part)
 
-    arrived = lax.all_gather(matched, "patch", axis=0, tiled=True)
+    arrived = ring_gather(matched, "patch", 0)
 
     def visit_one(offset, inner):
         hit_first = table[offset, 0] == own_patch

time: 676 us -> 744 us (1.10)
  starting transfers between devices: 10.8 us -> 101 us
  waiting for transfers between devices: 131 us -> 87 us
  local copies, waits for them, and re-layouts: 107 us -> 128 us
    all_gather x1 -> x0, waiting for transfers between devices: 101 us -> none  [local(): arrived = lax.all_gather(matched, 'patch', axis=0, tiled=True)]
    ppermute x0 -> x15, starting transfers between devices: none -> 90.3 us  [the longest x7 78.1 us: ring_gather(): later.append(lax.ppermute(later[-1], axis, down))]
    ppermute x0 -> x15, waiting for transfers between devices: none -> 46.9 us  [the longest x7 25.5 us: ring_gather(): later.append(lax.ppermute(later[-1], axis, down))]
    unnamed x24 -> x81, local copies, waits for them, and re-layouts: 2.04 us -> 17.1 us
    reduce_scatter x1, waiting for transfers between devices: 8.37 us -> 18.7 us  [local(): lax.psum_scatter(flux_sum, 'visit', scatter_dimension=0, tiled=True)]
  transfers between devices with their start and end apart: 7 -> 21, of which waited for: 5 -> 12; matrix products, arithmetic and copies ran while one was open for 0% -> 1% of each run, Pallas kernels for 0% -> 0%
where the time goes in v1:
time: 744 us; the launch traced here: 739 us
  loops' own time  185 us (25%)
  matrix products  141 us (19%)
  local copies, waits for them, and re-layouts  128 us (17%)
  starting transfers between devices  101 us (14%)
  waiting for transfers between devices  87 us (12%)
  other arithmetic  71.6 us (10%)
  between operations  26.1 us (4%)
    another operation x1, loops' own time, local(): flux_sum, cover_sum = lax.fori_loop(0, arrived.shape[0], visit_one, empty)  128 us
    dot_general x96, matrix products, match_exposure(): jnp.einsum('drw,xw->drx', smoothed[group, :count], col_band[group, x_degr...  108 us
    ppermute x7, starting transfers between devices, ring_gather(): later.append(lax.ppermute(later[-1], axis, down))  78.1 us
    dynamic_slice x96, local copies, waits for them, and re-layouts, visit_one(): hit_second = table[offset, 1] == own_patch  62.7 us
    another operation x96, loops' own time, visit_one(): lax.cond(hit_first | hit_second, lambda: add_exposure(inner, exposure, of...  56 us
    dot_general x15, matrix products, warp_exposure(): warped = jnp.dot(middle, col_map, preferred_element_type=jnp.float32)  28.8 us
    ppermute x7, waiting for transfers between devices, ring_gather(): later.append(lax.ppermute(later[-1], axis, down))  25.5 us
    ppermute x8, waiting for transfers between devices, ring_gather(): earlier.append(lax.ppermute(earlier[-1], axis, up))  21.4 us
  transfers between devices with their start and end apart: 21, of which 12 were waited for; matrix products, arithmetic and copies ran while one was open for 1% of the time, Pallas kernels for 0%

profile of v1, /device:TPU:5, one launch (start us, length us, event | category | flops | bytes accessed | tf_op | source)
XLA Modules:
  0.0 739.3 jit_solution(8303537450106149658)
XLA Ops:
  51.2 119.2 %while.28 = (s32[]{:T(128)}, bf16[6,128,512]{2,1,0:T(8,128)(2,1)S(1)}, f32[6,3,40]{2,1,0:T(4,128)S(1)}, bf16[6,128,512]{1,2,0:T(8,128)(2,1)S(1)}, bf16[4,4,128,1...) while((s32[]{:T(128)}, ...), condition=%wide.region_53.54_spmd.clone.clone, body=%wide.region_16.53_spmd.clone.clone.sunk | while | flops 2971667456 | bytes 70542368 | solution.py:136
  62.7 8.5 %fusion.219 = bf16[6,128,512]{2,1,0:T(8,128)(2,1)S(1)} fusion(bf16[6,128,512]{2,1,0:T(8,128)(2,1)S(1)} %get-tuple-element.857, s32[]{:T(128)} %get-tuple-element.856, bf16[4,4,512,512]{3,2,1,0:T(8,128)(2,1)S(1)} %copy-done, f32[128,512]{1,0:T(8,128)S(1)} %get-tuple-element.764, f32[128,512]{1,0:T(8,128)S(1)} %get-tuple-element.765, ...), kind=kOutput, calls=%fused_computation.133.clone.1 | convolution fusion | flops 73138176 | bytes 11012660 | tf_op jit(solution)/shard_map/while/body/eval_jaxpr/drw,xw->drx/dot_general | solution.py:65
  82.5 8.5 %fusion.219 = bf16[6,128,512]{2,1,0:T(8,128)(2,1)S(1)} fusion(bf16[6,128,512]{2,1,0:T(8,128)(2,1)S(1)} %get-tuple-element.857, s32[]{:T(128)} %get-tuple-element.856, bf16[4,4,512,512]{3,2,1,0:T(8,128)(2,1)S(1)} %copy-done, f32[128,512]{1,0:T(8,128)S(1)} %get-tuple-element.764, f32[128,512]{1,0:T(8,128)S(1)} %get-tuple-element.765, ...), kind=kOutput, calls=%fused_computation.133.clone.1 | convolution fusion | flops 73138176 | bytes 11012660 | tf_op jit(solution)/shard_map/while/body/eval_jaxpr/drw,xw->drx/dot_general | solution.py:65
  102.4 8.5 %fusion.219 = bf16[6,128,512]{2,1,0:T(8,128)(2,1)S(1)} fusion(bf16[6,128,512]{2,1,0:T(8,128)(2,1)S(1)} %get-tuple-element.857, s32[]{:T(128)} %get-tuple-element.856, bf16[4,4,512,512]{3,2,1,0:T(8,128)(2,1)S(1)} %copy-done, f32[128,512]{1,0:T(8,128)S(1)} %get-tuple-element.764, f32[128,512]{1,0:T(8,128)S(1)} %get-tuple-element.765, ...), kind=kOutput, calls=%fused_computation.133.clone.1 | convolution fusion | flops 73138176 | bytes 11012660 | tf_op jit(solution)/shard_map/while/body/eval_jaxpr/drw,xw->drx/dot_general | solution.py:65
  122.2 8.5 %fusion.219 = bf16[6,128,512]{2,1,0:T(8,128)(2,1)S(1)} fusion(bf16[6,128,512]{2,1,0:T(8,128)(2,1)S(1)} %get-tuple-element.857, s32[]{:T(128)} %get-tuple-element.856, bf16[4,4,512,512]{3,2,1,0:T(8,128)(2,1)S(1)} %copy-done, f32[128,512]{1,0:T(8,128)S(1)} %get-tuple-element.764, f32[128,512]{1,0:T(8,128)S(1)} %get-tuple-element.765, ...), kind=kOutput, calls=%fused_computation.133.clone.1 | convolution fusion | flops 73138176 | bytes 11012660 | tf_op jit(solution)/shard_map/while/body/eval_jaxpr/drw,xw->drx/dot_general | solution.py:65
  142.0 8.5 %fusion.219 = bf16[6,128,512]{2,1,0:T(8,128)(2,1)S(1)} fusion(bf16[6,128,512]{2,1,0:T(8,128)(2,1)S(1)} %get-tuple-element.857, s32[]{:T(128)} %get-tuple-element.856, bf16[4,4,512,512]{3,2,1,0:T(8,128)(2,1)S(1)} %copy-done, f32[128,512]{1,0:T(8,128)S(1)} %get-tuple-element.764, f32[128,512]{1,0:T(8,128)S(1)} %get-tuple-element.765, ...), kind=kOutput, calls=%fused_computation.133.clone.1 | convolution fusion | flops 73138176 | bytes 11012660 | tf_op jit(solution)/shard_map/while/body/eval_jaxpr/drw,xw->drx/dot_general | solution.py:65
  161.9 8.5 %fusion.219 = bf16[6,128,512]{2,1,0:T(8,128)(2,1)S(1)} fusion(bf16[6,128,512]{2,1,0:T(8,128)(2,1)S(1)} %get-tuple-element.857, s32[]{:T(128)} %get-tuple-element.856, bf16[4,4,512,512]{3,2,1,0:T(8,128)(2,1)S(1)} %copy-done, f32[128,512]{1,0:T(8,128)S(1)} %get-tuple-element.764, f32[128,512]{1,0:T(8,128)S(1)} %get-tuple-element.765, ...), kind=kOutput, calls=%fused_computation.133.clone.1 | convolution fusion | flops 73138176 | bytes 11012660 | tf_op jit(solution)/shard_map/while/body/eval_jaxpr/drw,xw->drx/dot_general | solution.py:65
  172.3 8.9 %collective-permute-done = bf16[6,128,512]{2,1,0:T(8,128)(2,1)S(1)} collective-permute-done((bf16[6,128,512]{2,1,0:T(8,128)(2,1)S(1)}, bf16[6,128,512]{2,1,0:T(8,128)(2,1)S(1)}, u32[]{:S(2)}, u32[]{:S(2)}) %collective-permute-start) | collective-permute-done | bytes 786464 | tf_op jit(solution)/shard_map/ppermute | solution.py:17
  184.6 9.0 %collective-permute-done.1 = bf16[6,128,512]{2,1,0:T(8,128)(2,1)S(1)} collective-permute-done((bf16[6,128,512]{2,1,0:T(8,128)(2,1)S(1)}, bf16[6,128,512]{2,1,0:T(8,128)(2,1)S(1)}, u32[]{:S(2)}, u32[]{:S(2)}) %collective-permute-start.1) | collective-permute-done | bytes 786464 | tf_op jit(solution)/shard_map/ppermute | solution.py:17
  212.5 15.6 %collective-permute-start.10 = (bf16[6,128,512]{2,1,0:T(8,128)(2,1)S(1)}, bf16[6,128,512]{2,1,0:T(8,128)(2,1)S(1)}, u32[]{:S(2)}, u32[]{:S(2)}) collective-permute-start(bf16[6,128,512]{2,1,0:T(8,128)(2,1)S(1)} %collective-permute-done.9), channel_id=1, source_target_pairs={{0,15},{1,0},{2,1},{3,2},{4,3},{5,4},{6,5},{7,6},{8,7},{9,8},{10,9... | collective-permute-start | bytes 2359304 | tf_op jit(solution)/shard_map/ppermute | solution.py:19
  233.6 14.3 %collective-permute-start.11 = (bf16[6,128,512]{2,1,0:T(8,128)(2,1)S(1)}, bf16[6,128,512]{2,1,0:T(8,128)(2,1)S(1)}, u32[]{:S(2)}, u32[]{:S(2)}) collective-permute-start(bf16[6,128,512]{2,1,0:T(8,128)(2,1)S(1)} %collective-permute-done.10), channel_id=1, source_target_pairs={{0,15},{1,0},{2,1},{3,2},{4,3},{5,4},{6,5},{7,6},{8,7},{9,8},{10,9... | collective-permute-start | bytes 2359304 | tf_op jit(solution)/shard_map/ppermute | solution.py:19
  254.3 14.3 %collective-permute-start.12 = (bf16[6,128,512]{2,1,0:T(8,128)(2,1)S(1)}, bf16[6,128,512]{2,1,0:T(8,128)(2,1)}, u32[]{:S(2)}, u32[]{:S(2)}) collective-permute-start(bf16[6,128,512]{2,1,0:T(8,128)(2,1)S(1)} %collective-permute-done.11), channel_id=1, source_target_pairs={{0,15},{1,0},{2,1},{3,2},{4,3},{5,4},{6,5},{7,6},{8,7},{9,8},{10,9... | collective-permute-start | bytes 2359304 | tf_op jit(solution)/shard_map/ppermute | solution.py:19
  274.3 14.2 %collective-permute-start.13 = (bf16[6,128,512]{2,1,0:T(8,128)(2,1)}, bf16[6,128,512]{2,1,0:T(8,128)(2,1)}, u32[]{:S(2)}, u32[]{:S(2)}) collective-permute-start(bf16[6,128,512]{2,1,0:T(8,128)(2,1)} %collective-permute-done.12), channel_id=1, source_target_pairs={{0,15},{1,0},{2,1},{3,2},{4,3},{5,4},{6,5},{7,6},{8,7},{9,8},{10,9... | collective-permute-start | bytes 2359304 | tf_op jit(solution)/shard_map/ppermute | solution.py:19
  294.4 14.3 %collective-permute-start.14 = (bf16[6,128,512]{2,1,0:T(8,128)(2,1)}, bf16[6,128,512]{2,1,0:T(8,128)(2,1)S(1)}, u32[]{:S(2)}, u32[]{:S(2)}) collective-permute-start(bf16[6,128,512]{2,1,0:T(8,128)(2,1)} %collective-permute-done.13), channel_id=1, source_target_pairs={{0,15},{1,0},{2,1},{3,2},{4,3},{5,4},{6,5},{7,6},{8,7},{9,8},{10,9... | collective-permute-start | bytes 2359304 | tf_op jit(solution)/shard_map/ppermute | solution.py:19
  329.7 335.8 %while.27 = (s32[]{:T(128)}, f32[128,512]{1,0:T(8,128)S(1)}, f32[128,512]{1,0:T(8,128)S(1)}, s32[96,2]{0,1:T(2,128)S(1)}, s32[]{:T(128)}, /*index=5*/f32[96]{0:T...) while((s32[]{:T(128)}, f32[128,512]{1,0:T(8,128)S(1)}, ...), condition=%wide.region_59.60_spmd, body=%wide.region_54.59_spmd.sunk | while | flops 88949520 | bytes 1204658 | solution.py:166
  339.7 9.6 %conditional.2 = ((f32[128,512]{1,0:T(8,128)S(1)}, f32[128,512]{1,0:T(8,128)S(1)})) conditional(s32[]{:T(128)} %convert_element_type.1283, (f32[128,512]{1,0:T(8,128)S(1)}, f32[128,512]{1,0:T(8,128)S(1)}) %tuple.161, (s32[]{:T(128)}, f32[96]{0:T(128)S(1)}, s32[96]{0:T(128)S(1)}, f32[96,2]{0,1:T(2,128)S(1)}, bf16[96,128,512]{2,1,0:T(8,128)(2,1)}, ...), branch_computations={%region_55.55_spmd, %region_56.58_spmd} | conditional | flops 88949512 | bytes 1204415 | solution.py:160
  375.2 9.6 %conditional.2 = ((f32[128,512]{1,0:T(8,128)S(1)}, f32[128,512]{1,0:T(8,128)S(1)})) conditional(s32[]{:T(128)} %convert_element_type.1283, (f32[128,512]{1,0:T(8,128)S(1)}, f32[128,512]{1,0:T(8,128)S(1)}) %tuple.161, (s32[]{:T(128)}, f32[96]{0:T(128)S(1)}, s32[96]{0:T(128)S(1)}, f32[96,2]{0,1:T(2,128)S(1)}, bf16[96,128,512]{2,1,0:T(8,128)(2,1)}, ...), branch_computations={%region_55.55_spmd, %region_56.58_spmd} | conditional | flops 88949512 | bytes 1204415 | solution.py:160
  394.8 9.6 %conditional.2 = ((f32[128,512]{1,0:T(8,128)S(1)}, f32[128,512]{1,0:T(8,128)S(1)})) conditional(s32[]{:T(128)} %convert_element_type.1283, (f32[128,512]{1,0:T(8,128)S(1)}, f32[128,512]{1,0:T(8,128)S(1)}) %tuple.161, (s32[]{:T(128)}, f32[96]{0:T(128)S(1)}, s32[96]{0:T(128)S(1)}, f32[96,2]{0,1:T(2,128)S(1)}, bf16[96,128,512]{2,1,0:T(8,128)(2,1)}, ...), branch_computations={%region_55.55_spmd, %region_56.58_spmd} | conditional | flops 88949512 | bytes 1204415 | solution.py:160
  414.4 9.6 %conditional.2 = ((f32[128,512]{1,0:T(8,128)S(1)}, f32[128,512]{1,0:T(8,128)S(1)})) conditional(s32[]{:T(128)} %convert_element_type.1283, (f32[128,512]{1,0:T(8,128)S(1)}, f32[128,512]{1,0:T(8,128)S(1)}) %tuple.161, (s32[]{:T(128)}, f32[96]{0:T(128)S(1)}, s32[96]{0:T(128)S(1)}, f32[96,2]{0,1:T(2,128)S(1)}, bf16[96,128,512]{2,1,0:T(8,128)(2,1)}, ...), branch_computations={%region_55.55_spmd, %region_56.58_spmd} | conditional | flops 88949512 | bytes 1204415 | solution.py:160
  434.0 9.6 %conditional.2 = ((f32[128,512]{1,0:T(8,128)S(1)}, f32[128,512]{1,0:T(8,128)S(1)})) conditional(s32[]{:T(128)} %convert_element_type.1283, (f32[128,512]{1,0:T(8,128)S(1)}, f32[128,512]{1,0:T(8,128)S(1)}) %tuple.161, (s32[]{:T(128)}, f32[96]{0:T(128)S(1)}, s32[96]{0:T(128)S(1)}, f32[96,2]{0,1:T(2,128)S(1)}, bf16[96,128,512]{2,1,0:T(8,128)(2,1)}, ...), branch_computations={%region_55.55_spmd, %region_56.58_spmd} | conditional | flops 88949512 | bytes 1204415 | solution.py:160
  451.6 9.6 %conditional.2 = ((f32[128,512]{1,0:T(8,128)S(1)}, f32[128,512]{1,0:T(8,128)S(1)})) conditional(s32[]{:T(128)} %convert_element_type.1283, (f32[128,512]{1,0:T(8,128)S(1)}, f32[128,512]{1,0:T(8,128)S(1)}) %tuple.161, (s32[]{:T(128)}, f32[96]{0:T(128)S(1)}, s32[96]{0:T(128)S(1)}, f32[96,2]{0,1:T(2,128)S(1)}, bf16[96,128,512]{2,1,0:T(8,128)(2,1)}, ...), branch_computations={%region_55.55_spmd, %region_56.58_spmd} | conditional | flops 88949512 | bytes 1204415 | solution.py:160
  473.2 9.6 %conditional.2 = ((f32[128,512]{1,0:T(8,128)S(1)}, f32[128,512]{1,0:T(8,128)S(1)})) conditional(s32[]{:T(128)} %convert_element_type.1283, (f32[128,512]{1,0:T(8,128)S(1)}, f32[128,512]{1,0:T(8,128)S(1)}) %tuple.161, (s32[]{:T(128)}, f32[96]{0:T(128)S(1)}, s32[96]{0:T(128)S(1)}, f32[96,2]{0,1:T(2,128)S(1)}, bf16[96,128,512]{2,1,0:T(8,128)(2,1)}, ...), branch_computations={%region_55.55_spmd, %region_56.58_spmd} | conditional | flops 88949512 | bytes 1204415 | solution.py:160
  494.8 9.6 %conditional.2 = ((f32[128,512]{1,0:T(8,128)S(1)}, f32[128,512]{1,0:T(8,128)S(1)})) conditional(s32[]{:T(128)} %convert_element_type.1283, (f32[128,512]{1,0:T(8,128)S(1)}, f32[128,512]{1,0:T(8,128)S(1)}) %tuple.161, (s32[]{:T(128)}, f32[96]{0:T(128)S(1)}, s32[96]{0:T(128)S(1)}, f32[96,2]{0,1:T(2,128)S(1)}, bf16[96,128,512]{2,1,0:T(8,128)(2,1)}, ...), branch_computations={%region_55.55_spmd, %region_56.58_spmd} | conditional | flops 88949512 | bytes 1204415 | solution.py:160
  522.4 9.6 %conditional.2 = ((f32[128,512]{1,0:T(8,128)S(1)}, f32[128,512]{1,0:T(8,128)S(1)})) conditional(s32[]{:T(128)} %convert_element_type.1283, (f32[128,512]{1,0:T(8,128)S(1)}, f32[128,512]{1,0:T(8,128)S(1)}) %tuple.161, (s32[]{:T(128)}, f32[96]{0:T(128)S(1)}, s32[96]{0:T(128)S(1)}, f32[96,2]{0,1:T(2,128)S(1)}, bf16[96,128,512]{2,1,0:T(8,128)(2,1)}, ...), branch_computations={%region_55.55_spmd, %region_56.58_spmd} | conditional | flops 88949512 | bytes 1204415 | solution.py:160
  543.9 9.6 %conditional.2 = ((f32[128,512]{1,0:T(8,128)S(1)}, f32[128,512]{1,0:T(8,128)S(1)})) conditional(s32[]{:T(128)} %convert_element_type.1283, (f32[128,512]{1,0:T(8,128)S(1)}, f32[128,512]{1,0:T(8,128)S(1)}) %tuple.161, (s32[]{:T(128)}, f32[96]{0:T(128)S(1)}, s32[96]{0:T(128)S(1)}, f32[96,2]{0,1:T(2,128)S(1)}, bf16[96,128,512]{2,1,0:T(8,128)(2,1)}, ...), branch_computations={%region_55.55_spmd, %region_56.58_spmd} | conditional | flops 88949512 | bytes 1204415 | solution.py:160
  569.5 9.6 %conditional.2 = ((f32[128,512]{1,0:T(8,128)S(1)}, f32[128,512]{1,0:T(8,128)S(1)})) conditional(s32[]{:T(128)} %convert_element_type.1283, (f32[128,512]{1,0:T(8,128)S(1)}, f32[128,512]{1,0:T(8,128)S(1)}) %tuple.161, (s32[]{:T(128)}, f32[96]{0:T(128)S(1)}, s32[96]{0:T(128)S(1)}, f32[96,2]{0,1:T(2,128)S(1)}, bf16[96,128,512]{2,1,0:T(8,128)(2,1)}, ...), branch_computations={%region_55.55_spmd, %region_56.58_spmd} | conditional | flops 88949512 | bytes 1204415 | solution.py:160
  585.1 9.6 %conditional.2 = ((f32[128,512]{1,0:T(8,128)S(1)}, f32[128,512]{1,0:T(8,128)S(1)})) conditional(s32[]{:T(128)} %convert_element_type.1283, (f32[128,512]{1,0:T(8,128)S(1)}, f32[128,512]{1,0:T(8,128)S(1)}) %tuple.161, (s32[]{:T(128)}, f32[96]{0:T(128)S(1)}, s32[96]{0:T(128)S(1)}, f32[96,2]{0,1:T(2,128)S(1)}, bf16[96,128,512]{2,1,0:T(8,128)(2,1)}, ...), branch_computations={%region_55.55_spmd, %region_56.58_spmd} | conditional | flops 88949512 | bytes 1204415 | solution.py:160
  610.7 9.6 %conditional.2 = ((f32[128,512]{1,0:T(8,128)S(1)}, f32[128,512]{1,0:T(8,128)S(1)})) conditional(s32[]{:T(128)} %convert_element_type.1283, (f32[128,512]{1,0:T(8,128)S(1)}, f32[128,512]{1,0:T(8,128)S(1)}) %tuple.161, (s32[]{:T(128)}, f32[96]{0:T(128)S(1)}, s32[96]{0:T(128)S(1)}, f32[96,2]{0,1:T(2,128)S(1)}, bf16[96,128,512]{2,1,0:T(8,128)(2,1)}, ...), branch_computations={%region_55.55_spmd, %region_56.58_spmd} | conditional | flops 88949512 | bytes 1204415 | solution.py:160
  626.3 9.6 %conditional.2 = ((f32[128,512]{1,0:T(8,128)S(1)}, f32[128,512]{1,0:T(8,128)S(1)})) conditional(s32[]{:T(128)} %convert_element_type.1283, (f32[128,512]{1,0:T(8,128)S(1)}, f32[128,512]{1,0:T(8,128)S(1)}) %tuple.161, (s32[]{:T(128)}, f32[96]{0:T(128)S(1)}, s32[96]{0:T(128)S(1)}, f32[96,2]{0,1:T(2,128)S(1)}, bf16[96,128,512]{2,1,0:T(8,128)(2,1)}, ...), branch_computations={%region_55.55_spmd, %region_56.58_spmd} | conditional | flops 88949512 | bytes 1204415 | solution.py:160
  651.9 9.6 %conditional.2 = ((f32[128,512]{1,0:T(8,128)S(1)}, f32[128,512]{1,0:T(8,128)S(1)})) conditional(s32[]{:T(128)} %convert_element_type.1283, (f32[128,512]{1,0:T(8,128)S(1)}, f32[128,512]{1,0:T(8,128)S(1)}) %tuple.161, (s32[]{:T(128)}, f32[96]{0:T(128)S(1)}, s32[96]{0:T(128)S(1)}, f32[96,2]{0,1:T(2,128)S(1)}, bf16[96,128,512]{2,1,0:T(8,128)(2,1)}, ...), branch_computations={%region_55.55_spmd, %region_56.58_spmd} | conditional | flops 88949512 | bytes 1204415 | solution.py:160
  668.3 18.7 %reduce-scatter.3.cloned.1.call-done = f32[64,512]{1,0:T(8,128)} async-done(((f32[128,512]{1,0:T(8,128)}), f32[64,512]{1,0:T(8,128)}) %reduce-scatter.3.cloned.1.call-update) | async-done | bytes 131088 | tf_op jit(solution)/shard_map/reduce_scatter | solution.py:168
  687.0 14.0 %reduce-scatter.5.cloned.1.call-done = f32[64,512]{1,0:T(8,128)} async-done(((f32[128,512]{1,0:T(8,128)}), f32[64,512]{1,0:T(8,128)}) %reduce-scatter.5.cloned.1.call-update) | async-done | bytes 131088 | tf_op jit(solution)/shard_map/reduce_scatter | solution.py:169
  (670 shorter events, 354.5 us)
Async XLA Ops:
  7.2 43.7 %copy-start.18 = (bf16[1,6,128,512]{3,2,1,0:T(8,128)(2,1)S(1)}, bf16[1,6,128,512]{3,2,1,0:T(8,128)(2,1)}, u32[]{:S(2)}) copy-start(bf16[1,6,128,512]{3,2,1,0:T(8,128)(2,1)} %param.13) | copy-start | bytes 2359300
  7.2 44.1 %copy-start.21 = (f32[1,6,3,40]{3,0,2,1:T(1,128)S(1)}, f32[1,6,3,40]{3,0,2,1:T(1,128)}, u32[]{:S(2)}) copy-start(f32[1,6,3,40]{3,0,2,1:T(1,128)} %param.14) | copy-start | bytes 8644
  7.2 679.8 %reduce-scatter.3.cloned.1.call-start = ((), (), s32[]{:S(2)}) async-start(), calls=%async_computation.2 | async-start | bytes 393216 | tf_op jit(solution)/shard_map/reduce_scatter | solution.py:168
  170.4 26.6 %copy-start.12 = (bf16[6,128,512]{2,1,0:T(8,128)(2,1)}, bf16[6,128,512]{2,1,0:T(8,128)(2,1)S(1)}, u32[]{:S(2)}) copy-start(bf16[6,128,512]{2,1,0:T(8,128)(2,1)S(1)} %get-tuple-element.365) | copy-start | bytes 2359300
  170.4 10.8 %collective-permute-start = (bf16[6,128,512]{2,1,0:T(8,128)(2,1)S(1)}, bf16[6,128,512]{2,1,0:T(8,128)(2,1)S(1)}, u32[]{:S(2)}, u32[]{:S(2)}) collective-permute-start(bf16[6,128,512]{2,1,0:T(8,128)(2,1)S(1)} %get-tuple-element.365), channel_id=1, source_target_pairs={{0,1},{1,2},{2,3},{3,4},{4,5},{5,6},{6,7},{7,8},{8,9},{9,10},{10,1... | collective-permute-start | bytes 2359304 | tf_op jit(solution)/shard_map/ppermute | solution.py:17
  181.2 12.4 %collective-permute-start.1 = (bf16[6,128,512]{2,1,0:T(8,128)(2,1)S(1)}, bf16[6,128,512]{2,1,0:T(8,128)(2,1)S(1)}, u32[]{:S(2)}, u32[]{:S(2)}) collective-permute-start(bf16[6,128,512]{2,1,0:T(8,128)(2,1)S(1)} %collective-permute-done), channel_id=1, source_target_pairs={{0,1},{1,2},{2,3},{3,4},{4,5},{5,6},{6,7},{7,8},{8,9},{9,10},{10,1... | collective-permute-start | bytes 2359304 | tf_op jit(solution)/shard_map/ppermute | solution.py:17
  184.6 12.4 %collective-permute-start.8 = (bf16[6,128,512]{2,1,0:T(8,128)(2,1)S(1)}, bf16[6,128,512]{2,1,0:T(8,128)(2,1)S(1)}, u32[]{:S(2)}, u32[]{:S(2)}) collective-permute-start(bf16[6,128,512]{2,1,0:T(8,128)(2,1)S(1)} %get-tuple-element.365), channel_id=1, source_target_pairs={{0,15},{1,0},{2,1},{3,2},{4,3},{5,4},{6,5},{7,6},{8,7},{9,8},{10,9... | collective-permute-start | bytes 2359304 | tf_op jit(solution)/shard_map/ppermute | solution.py:19
  193.6 12.4 %collective-permute-start.2 = (bf16[6,128,512]{2,1,0:T(8,128)(2,1)S(1)}, bf16[6,128,512]{2,1,0:T(8,128)(2,1)S(1)}, u32[]{:S(2)}, u32[]{:S(2)}) collective-permute-start(bf16[6,128,512]{2,1,0:T(8,128)(2,1)S(1)} %collective-permute-done.1), channel_id=1, source_target_pairs={{0,1},{1,2},{2,3},{3,4},{4,5},{5,6},{6,7},{7,8},{8,9},{9,10},{10,1... | collective-permute-start | bytes 2359304 | tf_op jit(solution)/shard_map/ppermute | solution.py:17
  197.0 15.4 %collective-permute-start.9 = (bf16[6,128,512]{2,1,0:T(8,128)(2,1)S(1)}, bf16[6,128,512]{2,1,0:T(8,128)(2,1)S(1)}, u32[]{:S(2)}, u32[]{:S(2)}) collective-permute-start(bf16[6,128,512]{2,1,0:T(8,128)(2,1)S(1)} %collective-permute-done.8), channel_id=1, source_target_pairs={{0,15},{1,0},{2,1},{3,2},{4,3},{5,4},{6,5},{7,6},{8,7},{9,8},{10,9... | collective-permute-start | bytes 2359304 | tf_op jit(solution)/shard_map/ppermute | solution.py:19
  206.0 27.6 %copy-start.2 = (bf16[6,128,512]{2,1,0:T(8,128)(2,1)}, bf16[6,128,512]{2,1,0:T(8,128)(2,1)S(1)}, u32[]{:S(2)}) copy-start(bf16[6,128,512]{2,1,0:T(8,128)(2,1)S(1)} %collective-permute-done.2) | copy-start | bytes 2359300
  206.0 22.0 %collective-permute-start.3 = (bf16[6,128,512]{2,1,0:T(8,128)(2,1)S(1)}, bf16[6,128,512]{2,1,0:T(8,128)(2,1)S(1)}, u32[]{:S(2)}, u32[]{:S(2)}) collective-permute-start(bf16[6,128,512]{2,1,0:T(8,128)(2,1)S(1)} %collective-permute-done.2), channel_id=1, source_target_pairs={{0,1},{1,2},{2,3},{3,4},{4,5},{5,6},{6,7},{7,8},{8,9},{9,10},{10,1... | collective-permute-start | bytes 2359304 | tf_op jit(solution)/shard_map/ppermute | solution.py:17
  212.5 21.1 %collective-permute-start.10 = (bf16[6,128,512]{2,1,0:T(8,128)(2,1)S(1)}, bf16[6,128,512]{2,1,0:T(8,128)(2,1)S(1)}, u32[]{:S(2)}, u32[]{:S(2)}) collective-permute-start(bf16[6,128,512]{2,1,0:T(8,128)(2,1)S(1)} %collective-permute-done.9), channel_id=1, source_target_pairs={{0,15},{1,0},{2,1},{3,2},{4,3},{5,4},{6,5},{7,6},{8,7},{9,8},{10,9... | collective-permute-start | bytes 2359304 | tf_op jit(solution)/shard_map/ppermute | solution.py:19
  228.0 46.2 %copy-start.8 = (bf16[6,128,512]{2,1,0:T(8,128)(2,1)}, bf16[6,128,512]{2,1,0:T(8,128)(2,1)S(1)}, u32[]{:S(2)}) copy-start(bf16[6,128,512]{2,1,0:T(8,128)(2,1)S(1)} %collective-permute-done.3) | copy-start | bytes 2359300
  228.0 19.8 %collective-permute-start.4 = (bf16[6,128,512]{2,1,0:T(8,128)(2,1)S(1)}, bf16[6,128,512]{2,1,0:T(8,128)(2,1)S(1)}, u32[]{:S(2)}, u32[]{:S(2)}) collective-permute-start(bf16[6,128,512]{2,1,0:T(8,128)(2,1)S(1)} %collective-permute-done.3), channel_id=1, source_target_pairs={{0,1},{1,2},{2,3},{3,4},{4,5},{5,6},{6,7},{7,8},{8,9},{9,10},{10,1... | collective-permute-start | bytes 2359304 | tf_op jit(solution)/shard_map/ppermute | solution.py:17
  233.6 19.8 %collective-permute-start.11 = (bf16[6,128,512]{2,1,0:T(8,128)(2,1)S(1)}, bf16[6,128,512]{2,1,0:T(8,128)(2,1)S(1)}, u32[]{:S(2)}, u32[]{:S(2)}) collective-permute-start(bf16[6,128,512]{2,1,0:T(8,128)(2,1)S(1)} %collective-permute-done.10), channel_id=1, source_target_pairs={{0,15},{1,0},{2,1},{3,2},{4,3},{5,4},{6,5},{7,6},{8,7},{9,8},{10,9... | collective-permute-start | bytes 2359304 | tf_op jit(solution)/shard_map/ppermute | solution.py:19
  247.9 40.6 %copy-start.10 = (bf16[6,128,512]{2,1,0:T(8,128)(2,1)}, bf16[6,128,512]{2,1,0:T(8,128)(2,1)S(1)}, u32[]{:S(2)}) copy-start(bf16[6,128,512]{2,1,0:T(8,128)(2,1)S(1)} %collective-permute-done.4) | copy-start | bytes 2359300
  247.9 20.7 %collective-permute-start.5 = (bf16[6,128,512]{2,1,0:T(8,128)(2,1)S(1)}, bf16[6,128,512]{2,1,0:T(8,128)(2,1)S(1)}, u32[]{:S(2)}, u32[]{:S(2)}) collective-permute-start(bf16[6,128,512]{2,1,0:T(8,128)(2,1)S(1)} %collective-permute-done.4), channel_id=1, source_target_pairs={{0,1},{1,2},{2,3},{3,4},{4,5},{5,6},{6,7},{7,8},{8,9},{9,10},{10,1... | collective-permute-start | bytes 2359304 | tf_op jit(solution)/shard_map/ppermute | solution.py:17
  254.3 19.9 %collective-permute-start.12 = (bf16[6,128,512]{2,1,0:T(8,128)(2,1)S(1)}, bf16[6,128,512]{2,1,0:T(8,128)(2,1)}, u32[]{:S(2)}, u32[]{:S(2)}) collective-permute-start(bf16[6,128,512]{2,1,0:T(8,128)(2,1)S(1)} %collective-permute-done.11), channel_id=1, source_target_pairs={{0,15},{1,0},{2,1},{3,2},{4,3},{5,4},{6,5},{7,6},{8,7},{9,8},{10,9... | collective-permute-start | bytes 2359304 | tf_op jit(solution)/shard_map/ppermute | solution.py:19
  268.6 19.9 %copy-start.14 = (bf16[6,128,512]{2,1,0:T(8,128)(2,1)}, bf16[6,128,512]{2,1,0:T(8,128)(2,1)S(1)}, u32[]{:S(2)}) copy-start(bf16[6,128,512]{2,1,0:T(8,128)(2,1)S(1)} %collective-permute-done.5) | copy-start | bytes 2359300
  268.6 19.8 %collective-permute-start.6 = (bf16[6,128,512]{2,1,0:T(8,128)(2,1)S(1)}, bf16[6,128,512]{2,1,0:T(8,128)(2,1)}, u32[]{:S(2)}, u32[]{:S(2)}) collective-permute-start(bf16[6,128,512]{2,1,0:T(8,128)(2,1)S(1)} %collective-permute-done.5), channel_id=1, source_target_pairs={{0,1},{1,2},{2,3},{3,4},{4,5},{5,6},{6,7},{7,8},{8,9},{9,10},{10,1... | collective-permute-start | bytes 2359304 | tf_op jit(solution)/shard_map/ppermute | solution.py:17
  274.3 20.2 %collective-permute-start.13 = (bf16[6,128,512]{2,1,0:T(8,128)(2,1)}, bf16[6,128,512]{2,1,0:T(8,128)(2,1)}, u32[]{:S(2)}, u32[]{:S(2)}) collective-permute-start(bf16[6,128,512]{2,1,0:T(8,128)(2,1)} %collective-permute-done.12), channel_id=1, source_target_pairs={{0,15},{1,0},{2,1},{3,2},{4,3},{5,4},{6,5},{7,6},{8,7},{9,8},{10,9... | collective-permute-start | bytes 2359304 | tf_op jit(solution)/shard_map/ppermute | solution.py:19
  288.5 20.3 %collective-permute-start.7 = (bf16[6,128,512]{2,1,0:T(8,128)(2,1)}, bf16[6,128,512]{2,1,0:T(8,128)(2,1)}, u32[]{:S(2)}, u32[]{:S(2)}) collective-permute-start(bf16[6,128,512]{2,1,0:T(8,128)(2,1)} %collective-permute-done.6), channel_id=1, source_target_pairs={{0,1},{1,2},{2,3},{3,4},{4,5},{5,6},{6,7},{7,8},{8,9},{9,10},{10,1... | collective-permute-start | bytes 2359304 | tf_op jit(solution)/shard_map/ppermute | solution.py:17
  288.6 26.3 %copy-start.3 = (bf16[6,128,512]{2,1,0:T(8,128)(2,1)S(1)}, bf16[6,128,512]{2,1,0:T(8,128)(2,1)}, u32[]{:S(2)}) copy-start(bf16[6,128,512]{2,1,0:T(8,128)(2,1)} %copy-done.2) | copy-start | bytes 2359300
  288.6 26.6 %copy-start.13 = (bf16[6,128,512]{2,1,0:T(8,128)(2,1)S(1)}, bf16[6,128,512]{2,1,0:T(8,128)(2,1)}, u32[]{:S(2)}) copy-start(bf16[6,128,512]{2,1,0:T(8,128)(2,1)} %copy-done.12) | copy-start | bytes 2359300
  288.6 26.9 %copy-start.5 = (bf16[6,128,512]{2,1,0:T(8,128)(2,1)S(1)}, bf16[6,128,512]{2,1,0:T(8,128)(2,1)}, u32[]{:S(2)}) copy-start(bf16[6,128,512]{2,1,0:T(8,128)(2,1)} %copy-done.4) | copy-start | bytes 2359300
  294.4 23.8 %collective-permute-start.14 = (bf16[6,128,512]{2,1,0:T(8,128)(2,1)}, bf16[6,128,512]{2,1,0:T(8,128)(2,1)S(1)}, u32[]{:S(2)}, u32[]{:S(2)}) collective-permute-start(bf16[6,128,512]{2,1,0:T(8,128)(2,1)} %collective-permute-done.13), channel_id=1, source_target_pairs={{0,15},{1,0},{2,1},{3,2},{4,3},{5,4},{6,5},{7,6},{8,7},{9,8},{10,9... | collective-permute-start | bytes 2359304 | tf_op jit(solution)/shard_map/ppermute | solution.py:19
  666.2 34.7 %reduce-scatter.5.cloned.1.call-start = ((), (), s32[]{:S(2)}) async-start(), calls=%async_computation.3 | async-start | bytes 393216 | tf_op jit(solution)/shard_map/reduce_scatter | solution.py:169
  702.0 30.5 %copy-start.16 = (f32[64,512]{1,0:T(8,128)}, f32[64,512]{1,0:T(8,128)S(1)}, u32[]{:S(2)}) copy-start(f32[64,512]{1,0:T(8,128)S(1)} %maximum_divide_fusion) | copy-start | bytes 393220
  702.0 3.5 collective-permute-start.15
  704.2 4.4 collective-permute-start.16
  708.7 7.9 %collective-permute-start.17 = (f32[72,4]{1,0:T(8,128)S(1)}, f32[72,4]{1,0:T(8,128)S(1)}, u32[]{:S(2)}, u32[]{:S(2)}) collective-permute-start(f32[72,4]{1,0:T(8,128)S(1)} %get-tuple-element.558), channel_id=1, source_target_pairs={{0,1},{1,2},{2,3},{3,4},{4,5},{5,6},{6,7},{7,8},{8,9},{9,10},{10,1... | collective-permute-start | bytes 3464 | tf_op jit(solution)/shard_map/ppermute | solution.py:31
  713.9 6.2 collective-permute-start.18
  (19 other events, 94.9 us)
Sparse Core Ops, SparseCore 0:
  666.3 20.5 reduce-scatter.2
  689.2 11.7 reduce-scatter.4
